TPU v7x, 256 devices: a whole 4x4x8 slice. The times are simulated.
256 devices in a mesh: cls: 2 (over y_hi), dom: 16 (over y_lo, x, core), orient: 8 (over z).
Axes of the slice: x: 4, y: 4 (y_hi: 2, y_lo: 2; y = y_hi * 2 + y_lo), z: 8, core: 2. Of those that a mesh axis runs over, the one named last changes fastest.
Arguments:
- references: bfloat16 [2, 8, 8, 32768], P(None, 'cls', None, ('dom', 'orient')), may hold values from -2 to 2
- images: bfloat16 [2, 2048, 32768], P(None, ('dom', 'orient')), may hold values from -16 to 16
- orient_lists: int32 [2048, 1], P(('dom', 'orient')), may hold values from 0 to 7; in each aligned block of 16 rows (0 to 15, 16 to 31, ...) at most 3 rows name the same one
- shift_ids: int32 [2048, 1], P(('dom', 'orient')), may hold values from 0 to 63
- fixed_weights: float32 [2048, 1], P(('dom', 'orient')), may hold values from 0.2 to 2
Outputs:
- class_prob: float32 [2048, 8], P(('dom', 'orient'), 'cls')
- volume: float32 [2, 8, 8, 32768], P(None, 'cls', 'orient', 'dom')
Inputs may be any that keep to these rules, and one draw needn't show every extreme that they name: `orient_lists`: within the rows of one device (16 particles), no orientation bin is listed by more than 3 particles, a bound that some block reaches.
All inputs are finite; a program needn't handle non-finite values.
Results may differ from a plain program's by a relative error of at most 0.02.
Values may be sent and summed in bfloat16 or wider, within the bound.
A program may use at most 320 MiB of HBM per device.

v0:
```python
import math
import jax
import jax.numpy as jnp
from jax import lax
from jax.sharding import PartitionSpec as P

IMG = 256
TX = 8
TY = 8
TWO_PI = 2.0 * math.pi


def offsets(number):
    return (jnp.arange(number, dtype=jnp.int32) - number // 2).astype(jnp.float32)


def local(references, images, orient_lists, shift_ids, fixed_weights):
    here = images.shape[1]
    classes, orients = (references.shape[1], references.shape[2])
    doms = lax.axis_size("dom")
    band = images.shape[2] // doms
    particles = here * doms
    held = lax.all_to_all(images, "dom", split_axis=2, concat_axis=1, tiled=True)
    piece = lax.all_gather(references, "orient", axis=3, tiled=True)
    ids = lax.all_gather(
        jnp.concatenate([orient_lists, shift_ids], axis=1), "dom", axis=0, tiled=True
    )
    orient_ids, shift_index = (ids[:, 0], ids[:, 1])
    columns = jnp.arange(band, dtype=jnp.int32) + lax.axis_index("dom") * band
    freq_x = (columns % IMG - IMG // 2).astype(jnp.float32)
    freq_y = (columns // IMG).astype(jnp.float32)
    angle_x = TWO_PI / IMG * (offsets(TX)[:, None] * freq_x[None, :])
    angle_y = TWO_PI / IMG * (offsets(TY)[:, None] * freq_y[None, :])
    cx, sx, cy, sy = (jnp.cos(angle_x), jnp.sin(angle_x), jnp.cos(angle_y), jnp.sin(angle_y))
    re, im = (held[0].astype(jnp.float32), held[1].astype(jnp.float32))
    x_re = (re[:, None] * cx - im[:, None] * sx).astype(jnp.bfloat16).reshape(particles * TX, band)
    x_im = (re[:, None] * sx + im[:, None] * cx).astype(jnp.bfloat16).reshape(particles * TX, band)
    r_re = piece[0].reshape(classes * orients, band).astype(jnp.float32)
    r_im = piece[1].reshape(classes * orients, band).astype(jnp.float32)
    s_re = (r_re[None] * cy[:, None] + r_im[None] * sy[:, None]).astype(jnp.bfloat16)
    s_im = (r_im[None] * cy[:, None] - r_re[None] * sy[:, None]).astype(jnp.bfloat16)
    s_re = s_re.reshape(TY * classes * orients, band)
    s_im = s_im.reshape(TY * classes * orients, band)
    part = jnp.einsum("aj,bj->ab", x_re, s_re, preferred_element_type=jnp.float32)
    part = part + jnp.einsum("aj,bj->ab", x_im, s_im, preferred_element_type=jnp.float32)
    part = lax.all_to_all(
        part.reshape(doms, here * TX, -1), "dom", split_axis=0, concat_axis=0, tiled=True
    )
    logits = jnp.sum(part, axis=0).reshape(here, TX, TY, classes, orients)
    top = jnp.max(logits, axis=(1, 2, 3, 4))
    top = lax.pmax(top, "cls")
    exponent = jnp.exp(logits - top[:, None, None, None, None])
    sums = jnp.sum(exponent, axis=(1, 2, 4))
    totals = lax.psum(jnp.sum(sums, axis=1), "cls")
    class_prob = sums / totals[:, None]
    weight = (fixed_weights * class_prob).astype(jnp.bfloat16)
    weight = lax.all_gather(weight, "dom", axis=0, tiled=True)
    entry_x = (shift_index % TX - TX // 2).astype(jnp.float32)
    entry_y = (shift_index // TX - TY // 2).astype(jnp.float32)
    angle = TWO_PI / IMG * (entry_x[:, None] * freq_x[None] + entry_y[:, None] * freq_y[None])
    cosine, sine = (jnp.cos(angle), jnp.sin(angle))
    row_re = (re * cosine - im * sine).astype(jnp.bfloat16)
    row_im = (re * sine + im * cosine).astype(jnp.bfloat16)
    onehot = (orient_ids[:, None] == jnp.arange(orients, dtype=jnp.int32)[None]).astype(
        jnp.bfloat16
    )
    mixing = (onehot[:, :, None] * weight[:, None, :]).reshape(particles, orients * classes)
    grown = [
        jnp.einsum("pm,pj->mj", mixing, row, preferred_element_type=jnp.float32).reshape(
            orients, 1, classes, band
        )
        for row in (row_re, row_im)
    ]
    grown = jnp.concatenate(grown, axis=1)
    grown = lax.all_to_all(grown, "orient", split_axis=0, concat_axis=0, tiled=True)
    volume = jnp.sum(grown, axis=0)[:, :, None, :]
    return (class_prob, volume)


def solution(mesh):
    in_specs = (
        P(None, "cls", None, ("dom", "orient")),
        P(None, ("dom", "orient"), None),
        P(("dom", "orient"), None),
        P(("dom", "orient"), None),
        P(("dom", "orient"), None),
    )
    out_specs = (P(("dom", "orient"), "cls"), P(None, "cls", "orient", "dom"))
    return jax.shard_map(local, mesh=mesh, in_specs=in_specs, out_specs=out_specs, check_vma=False)
```

profile of v0, /device:TPU:1, one launch (start us, length us, event | category | flops | bytes accessed | tf_op | source)
XLA Modules:
  0.0 253.7 jit_solution(4576734842398924274)
XLA Ops:
  0.6 30.9 %copy.31 = bf16[2,16,32768]{1,0,2:T(2,128)(2,1)} copy(bf16[2,16,32768]{2,1,0:T(8,128)(2,1)} %param.6) | data formatting | bytes 4194304 | tf_op args[1]
  31.5 20.8 %reshape.408 = bf16[16,2,32768]{2,1,0:T(2,128)(2,1)} reshape(bf16[32768,2,16]{2,1,0:T(2,128)(2,1)} %bitcast.57) | data formatting | bytes 4194304
  52.3 0.0 copy-start.1
  52.3 7.0 %all-to-all-start = ((bf16[16,2,32768]{2,1,0:T(2,128)(2,1)}), bf16[16,2,32768]{2,1,0:T(2,128)(2,1)S(1)}, u32[]{:S(2)}, u32[]{:S(2)}) async-start(bf16[16,2,32768]{2,1,0:T(2,128)(2,1)} %reshape.408), calls=%async_computation | async-start | bytes 4194304 | tf_op jit(solution)/shard_map/all_to_all | solution.py:23
  59.3 0.0 copy-done.1
  59.3 24.1 %all_gather.9 = bf16[2,4,8,2048]{3,2,1,0:T(8,128)(2,1)S(1)} all-gather(bf16[2,4,8,256]{3,2,1,0:T(8,128)(2,1)S(1)} %copy-done.1), channel_id=1, replica_groups=mesh['cls'=2,'dom'=16,'orient'=8] {'orient'}, dimensions={3}, use_global_device_ids=true | all-gather | bytes 294912 | tf_op jit(solution)/shard_map/all_gather | solution.py:24
  83.5 0.5 fusion.24
  84.0 1.5 subtract_convert_fusion.2
  85.6 1.3 all-to-all-done
  86.9 14.4 %reshape.409 = bf16[32768,2,16]{2,1,0:T(2,128)(2,1)} reshape(bf16[16,2,32768]{2,1,0:T(2,128)(2,1)S(1)} %all-to-all-done) | data formatting | bytes 4194304
  101.3 23.3 %copy.45 = bf16[2,16,16,2048]{3,2,1,0:T(8,128)(2,1)S(1)} copy(bf16[2,16,16,2048]{1,0,3,2:T(2,128)(2,1)} %bitcast.56) | data formatting | bytes 4194304 | tf_op jit(solution)/shard_map/all_to_all | solution.py:23
  124.6 0.5 slice_convert_fusion.1
  125.2 1.2 copy.33
  126.4 0.0 copy-start
  126.4 1.2 copy.34
  127.6 0.0 copy-done
  127.6 2.8 %fusion.1 = f32[2048,256]{1,0:T(8,128)S(1)} fusion(bf16[256,2048]{1,0:T(8,128)(2,1)S(1)} %bitcast.68, f32[8,2048]{1,0:T(8,128)S(1)} %get-tuple-element.15, f32[256,2048]{1,0:T(8,128)S(1)} %bitcast.65, f32[8,2048]{1,0:T(8,128)S(1)} %get-tuple-element.14, f32[256,2048]{1,0:T(8,128)S(1)} %bitcast.63), kind=kOutput, calls=%fused_computation.3 | convolution fusion | flops 2164260864 | bytes 7471104 | tf_op jit(solution)/shard_map/aj,bj->ab/dot_general | solution.py:44
  130.4 3.9 %fusion.14 = f32[2048,256]{1,0:T(8,128)} fusion(f32[2048,256]{1,0:T(8,128)S(1)} %fusion.1, bf16[256,2048]{1,0:T(8,128)(2,1)S(1)} %bitcast.67, f32[8,2048]{1,0:T(8,128)S(1)} %get-tuple-element.15, f32[256,2048]{1,0:T(8,128)S(1)} %bitcast.66, f32[8,2048]{1,0:T(8,128)S(1)} %get-tuple-element.14, f32[256,2048]{1,0:T(8,128)S(1)} %bitcast.64), kind=kOutput, calls=%fused_computation.14 | convolution fusion | flops 2164785152 | bytes 9568256 | tf_op jit(solution)/shard_map/aj,bj->ab/dot_general | solution.py:45
  134.3 0.0 copy-start.3
  134.3 0.0 copy-start.4
  134.3 8.8 %all-to-all-start.1 = ((f32[16,128,256]{2,1,0:T(8,128)}), f32[16,128,256]{2,1,0:T(8,128)}, u32[]{:S(2)}, u32[]{:S(2)}) async-start(f32[16,128,256]{2,1,0:T(8,128)} %bitcast.62), calls=%async_computation.1 | async-start | bytes 4194304 | tf_op jit(solution)/shard_map/all_to_all | solution.py:46
  143.1 0.0 copy-done.3
  143.1 0.0 copy-done.4
  143.1 40.1 %all-gather = s32[16,16,2]{1,2,0:T(2,128)S(1)} all-gather(s32[1,16,2]{1,2,0:T(2,128)S(1)} %add_bitcast_fusion), channel_id=1, replica_groups=mesh['cls'=2,'dom'=16,'orient'=8] {'dom'}, dimensions={0}, use_global_device_ids=true | all-gather | bytes 2176 | tf_op jit(solution)/shard_map/all_gather | solution.py:25
  183.3 0.1 reshape.391
  183.4 0.1 mul.358
  183.5 0.1 copy.38
  183.5 0.1 mul.362
  183.6 0.1 copy.39
  183.7 8.7 %subtract_convert_fusion.1 = (bf16[1,16,16,2048]{3,1,2,0:T(8,128)(2,1)S(1)}, bf16[1,16,16,2048]{3,1,2,0:T(8,128)(2,1)S(1)}) fusion(f32[2048]{0:T(1024)S(1)} %get-tuple-element.23, f32[16,16]{0,1:T(8,128)S(1)} %copy.39, f32[2048]{0:T(1024)S(1)} %get-tuple-element.22, f32[16,16]{0,1:T(8,128)S(1)} %copy.38, bf16[2,16,16,2048]{3,1,2,0:T(8,128)(2,1)S(1)} %bitcast.59), kind=kLoop, calls=%fused_computation.18 | loop fusion | flops 7340032 | bytes 4212736 | tf_op jit(solution)/shard_map/convert_element_type | solution.py:62
  192.4 0.6 copy.40
  193.0 1.6 copy.42
  194.6 0.0 all-to-all-done.1
  194.6 1.7 reduce_sum.43
  196.3 0.1 copy.35
  196.4 0.1 reduce_max.10
  196.5 0.1 reduce_max.14
  196.6 0.1 reduce_max.18
  196.7 5.3 %pmax.7 = f32[16]{0:T(128)S(1)} all-reduce(f32[16]{0:T(128)S(1)} %reduce_max.18), channel_id=1, replica_groups=mesh['cls'=2,'dom'=16,'orient'=8] {'cls'}, use_global_device_ids=true, to_apply=%region_3.4 | all-reduce | flops 16 | bytes 128 | tf_op jit(solution)/shard_map/pmax | solution.py:51
  202.0 0.1 sub.78
  202.1 0.1 sub.79
  202.2 0.2 exponential_reduce_fusion.1
  202.4 0.1 reduce_sum.46
  202.5 0.1 reduce_sum.47
  202.6 5.3 %psum.7 = f32[16]{0:T(128)S(1)} all-reduce(f32[16]{0:T(128)S(1)} %reduce_sum.47), channel_id=1, replica_groups=mesh['cls'=2,'dom'=16,'orient'=8] {'cls'}, use_global_device_ids=true, to_apply=%region_7.8 | all-reduce | flops 16 | bytes 128 | tf_op jit(solution)/shard_map/psum | solution.py:54
  207.9 0.0 copy-start.2
  207.9 1.1 reshape.384
  209.0 0.5 exponential_reduce_fusion
  209.5 0.0 copy-done.2
  209.5 0.6 fusion.36
  210.1 18.2 %all-gather.1 = bf16[16,16,4]{1,2,0:T(4,128)(2,1)S(1)} all-gather(bf16[1,16,4]{1,2,0:T(4,128)(2,1)S(1)} %get-tuple-element.4), channel_id=1, replica_groups=mesh['cls'=2,'dom'=16,'orient'=8] {'dom'}, dimensions={0}, use_global_device_ids=true | all-gather | bytes 2176 | tf_op jit(solution)/shard_map/all_gather | solution.py:57
  228.4 0.1 reshape.393
  228.6 0.3 convolution_bitcast_fusion.1
  228.8 1.5 convolution_bitcast_fusion
  230.4 0.3 copy.44
  230.7 22.2 %all_to_all.25 = f32[8,2,4,2048]{3,2,1,0:T(4,128)S(1)} all-to-all(f32[8,2,4,2048]{3,2,1,0:T(4,128)S(1)} %copy.44), channel_id=1, replica_groups=mesh['cls'=2,'dom'=16,'orient'=8] {'orient'}, dimensions={0} | all-to-all | bytes 1048576 | tf_op jit(solution)/shard_map/all_to_all | solution.py:75
  253.0 0.1 reduce_sum.48
  253.1 0.7 broadcast_in_dim.2
  (13 shorter events, 0.2 us)
Async XLA Ops:
  52.3 7.0 %copy-start.1 = (bf16[2,4,8,256]{3,2,1,0:T(8,128)(2,1)S(1)}, bf16[2,4,8,256]{3,2,1,0:T(8,128)(2,1)}, u32[]{:S(2)}) copy-start(bf16[2,4,8,256]{3,2,1,0:T(8,128)(2,1)} %param.5) | copy-start | bytes 98308
  52.3 34.6 %all-to-all-start = ((bf16[16,2,32768]{2,1,0:T(2,128)(2,1)}), bf16[16,2,32768]{2,1,0:T(2,128)(2,1)S(1)}, u32[]{:S(2)}, u32[]{:S(2)}) async-start(bf16[16,2,32768]{2,1,0:T(2,128)(2,1)} %reshape.408), calls=%async_computation | async-start | bytes 4194304 | tf_op jit(solution)/shard_map/all_to_all | solution.py:23
  126.4 1.2 copy-start
  134.3 8.8 %copy-start.3 = (s32[16,1]{0,1:T(1,128)S(1)}, s32[16,1]{0,1:T(1,128)}, u32[]{:S(2)}) copy-start(s32[16,1]{0,1:T(1,128)} %param.8) | copy-start | bytes 196
  134.3 8.8 %copy-start.4 = (s32[16,1]{0,1:T(1,128)S(1)}, s32[16,1]{0,1:T(1,128)}, u32[]{:S(2)}) copy-start(s32[16,1]{0,1:T(1,128)} %param.7) | copy-start | bytes 196
  134.3 60.3 %all-to-all-start.1 = ((f32[16,128,256]{2,1,0:T(8,128)}), f32[16,128,256]{2,1,0:T(8,128)}, u32[]{:S(2)}, u32[]{:S(2)}) async-start(f32[16,128,256]{2,1,0:T(8,128)} %bitcast.62), calls=%async_computation.1 | async-start | bytes 4194304 | tf_op jit(solution)/shard_map/all_to_all | solution.py:46
  207.9 1.6 copy-start.2
where the time goes:
time: 258 us; the launch traced here: 254 us
  blocking collectives  115 us (45%)
  local copies, waits for them, and re-layouts  97 us (38%)
  starting transfers between devices  15.7 us (6%)
  other arithmetic  15 us (6%)
  matrix products  8.47 us (3%)
    unnamed x15, local copies, waits for them, and re-layouts  66.2 us
    all_gather x1, blocking collectives, local(): lax.all_gather(jnp.concatenate([orient_lists, shift_ids], axis=1), 'dom',...  40.1 us
    all_gather x1, blocking collectives, local(): piece = lax.all_gather(references, 'orient', axis=3, tiled=True)  24.1 us
    all_to_all x1, local copies, waits for them, and re-layouts, local(): lax.all_to_all(images, 'dom', split_axis=2, concat_axis=1, tiled=True)  23.3 us
    all_to_all x1, blocking collectives, local(): lax.all_to_all(grown, 'orient', split_axis=0, concat_axis=0, tiled=True)  22.2 us
    all_gather x1, blocking collectives, local(): weight = lax.all_gather(weight, 'dom', axis=0, tiled=True)  18.2 us
    all_to_all x1, starting transfers between devices, local(): lax.all_to_all(part.reshape(doms, here * TX, -1), 'dom', split_axis=0, co...  8.77 us
    convert_element_type x1, other arithmetic, local(): row_re = (re * cosine - im * sine).astype(jnp.bfloat16)  8.74 us
  transfers between devices with their start and end apart: 2, of which 1 were waited for; matrix products, arithmetic and copies ran while one was open for 5% of the time, Pallas kernels for 0%

commit v1 on v0

--- a/solution.py
+++ b/solution.py
@@ -21,7 +21,9 @@
     band = images.shape[2] // doms
     particles = here * doms
     held = lax.all_to_all(images, "dom", split_axis=2, concat_axis=1, tiled=True)
-    piece = lax.all_gather(references, "orient", axis=3, tiled=True)
+    piece = jnp.concatenate(
+        lax.all_to_all(jnp.stack([references] * lax.axis_size("orient")), "orient", 0, 0), axis=3
+    )
     ids = lax.all_gather(
         jnp.concatenate([orient_lists, shift_ids], axis=1), "dom", axis=0, tiled=True
     )

time: 258 us -> 267 us (1.035)
  waiting for transfers between devices: 1.35 us -> 25 us
  blocking collectives: 115 us -> 93.6 us
  starting transfers between devices: 15.7 us -> 20.4 us
    all_gather x1 -> x0, blocking collectives: 24.1 us -> none  [local(): piece = lax.all_gather(references, 'orient', axis=3, tiled=True)]
    all_to_all x1, waiting for transfers between devices: 1.35 us -> 25 us  [local(): lax.all_to_all(images, 'dom', split_axis=2, concat_axis=1, tiled=True)]
    all_to_all x0 -> x1, starting transfers between devices: none -> 9.01 us  [local(): lax.all_to_all(jnp.stack([references] * lax.axis_size('orient')), 'orient...]
    all_to_all x1, starting transfers between devices: 8.77 us -> 5.08 us  [local(): lax.all_to_all(part.reshape(doms, here * TX, -1), 'dom', split_axis=0, co...]
    unnamed x15 -> x16, local copies, waits for them, and re-layouts: 66.2 us -> 66.7 us
  transfers between devices with their start and end apart: 2 -> 3, of which waited for: 1 -> 1; matrix products, arithmetic and copies ran while one was open for 5% -> 25% of each run, Pallas kernels for 0% -> 0%
where the time goes in v1:
time: 267 us; the launch traced here: 262 us
  local copies, waits for them, and re-layouts  99 us (37%)
  blocking collectives  93.6 us (35%)
  waiting for transfers between devices  25 us (9%)
  starting transfers between devices  20.4 us (8%)
  other arithmetic  15 us (6%)
  matrix products  8.47 us (3%)
    unnamed x16, local copies, waits for them, and re-layouts  66.7 us
    all_gather x1, blocking collectives, local(): lax.all_gather(jnp.concatenate([orient_lists, shift_ids], axis=1), 'dom',...  40.1 us
    all_to_all x1, waiting for transfers between devices, local(): lax.all_to_all(images, 'dom', split_axis=2, concat_axis=1, tiled=True)  25 us
    all_to_all x1, blocking collectives, local(): lax.all_to_all(grown, 'orient', split_axis=0, concat_axis=0, tiled=True)  24.6 us
    all_to_all x1, local copies, waits for them, and re-layouts, local(): lax.all_to_all(images, 'dom', split_axis=2, concat_axis=1, tiled=True)  23.3 us
    all_gather x1, blocking collectives, local(): weight = lax.all_gather(weight, 'dom', axis=0, tiled=True)  18.2 us
    all_to_all x1, starting transfers between devices, local(): lax.all_to_all(jnp.stack([references] * lax.axis_size('orient')), 'orient...  9.01 us
    convert_element_type x1, other arithmetic, local(): row_re = (re * cosine - im * sine).astype(jnp.bfloat16)  8.74 us
  transfers between devices with their start and end apart: 3, of which 1 were waited for; matrix products, arithmetic and copies ran while one was open for 25% of the time, Pallas kernels for 0%

profile of v1, /device:TPU:1, one launch (start us, length us, event | category | flops | bytes accessed | tf_op | source)
XLA Modules:
  0.0 262.2 jit_solution(13225554381849066761)
XLA Ops:
  0.6 1.5 stack.2
  2.1 9.0 %all-to-all-start.1 = ((bf16[8,2,4,8,256]{4,3,2,1,0:T(8,128)(2,1)}), bf16[8,2,4,8,256]{4,3,2,1,0:T(8,128)(2,1)S(1)}, u32[]{:S(2)}, u32[]{:S(2)}) async-start(bf16[8,2,4,8,256]{4,3,2,1,0:T(8,128)(2,1)} %stack.2), calls=%async_computation.1 | async-start | bytes 524288 | tf_op jit(solution)/shard_map/all_to_all | solution.py:25
  11.1 30.9 %copy.31 = bf16[2,16,32768]{1,0,2:T(2,128)(2,1)} copy(bf16[2,16,32768]{2,1,0:T(8,128)(2,1)} %param.6) | data formatting | bytes 4194304 | tf_op args[1]
  42.0 20.8 %reshape.419 = bf16[16,2,32768]{2,1,0:T(2,128)(2,1)} reshape(bf16[32768,2,16]{2,1,0:T(2,128)(2,1)} %bitcast.56) | data formatting | bytes 4194304
  62.8 0.0 all-to-all-done.1
  62.8 6.3 %all-to-all-start = ((bf16[16,2,32768]{2,1,0:T(2,128)(2,1)}), bf16[16,2,32768]{2,1,0:T(2,128)(2,1)S(1)}, u32[]{:S(2)}, u32[]{:S(2)}) async-start(bf16[16,2,32768]{2,1,0:T(2,128)(2,1)} %reshape.419), calls=%async_computation | async-start | bytes 4194304 | tf_op jit(solution)/shard_map/all_to_all | solution.py:23
  69.1 0.5 fusion.22
  69.7 0.3 copy_bitcast_fusion
  70.0 0.1 copy.48
  70.1 0.1 copy.49
  70.2 1.5 subtract_convert_fusion.2
  71.8 25.0 %all-to-all-done = bf16[16,2,32768]{2,1,0:T(2,128)(2,1)S(1)} async-done(((bf16[16,2,32768]{2,1,0:T(2,128)(2,1)}), bf16[16,2,32768]{2,1,0:T(2,128)(2,1)S(1)}, u32[]{:S(2)}, u32[]{:S(2)}) %all-to-all-start) | async-done | bytes 2097184 | tf_op jit(solution)/shard_map/all_to_all | solution.py:23
  96.8 14.4 %reshape.420 = bf16[32768,2,16]{2,1,0:T(2,128)(2,1)} reshape(bf16[16,2,32768]{2,1,0:T(2,128)(2,1)S(1)} %all-to-all-done) | data formatting | bytes 4194304
  111.2 23.3 %copy.47 = bf16[2,16,16,2048]{3,2,1,0:T(8,128)(2,1)S(1)} copy(bf16[2,16,16,2048]{1,0,3,2:T(2,128)(2,1)} %bitcast.55) | data formatting | bytes 4194304 | tf_op jit(solution)/shard_map/all_to_all | solution.py:23
  134.5 0.5 slice_convert_fusion.1
  135.0 1.2 copy.33
  136.2 0.0 copy-start
  136.2 1.2 copy.34
  137.5 0.0 copy-done
  137.5 2.8 %fusion.1 = f32[2048,256]{1,0:T(8,128)S(1)} fusion(bf16[256,2048]{1,0:T(8,128)(2,1)S(1)} %bitcast.68, f32[8,2048]{1,0:T(8,128)S(1)} %get-tuple-element.15, f32[256,2048]{1,0:T(8,128)S(1)} %bitcast.64, f32[8,2048]{1,0:T(8,128)S(1)} %get-tuple-element.14, f32[256,2048]{1,0:T(8,128)S(1)} %bitcast.62), kind=kOutput, calls=%fused_computation.3 | convolution fusion | flops 2164260864 | bytes 7471104 | tf_op jit(solution)/shard_map/aj,bj->ab/dot_general | solution.py:46
  140.2 3.9 %fusion.14 = f32[2048,256]{1,0:T(8,128)} fusion(f32[2048,256]{1,0:T(8,128)S(1)} %fusion.1, bf16[256,2048]{1,0:T(8,128)(2,1)S(1)} %bitcast.67, f32[8,2048]{1,0:T(8,128)S(1)} %get-tuple-element.15, f32[256,2048]{1,0:T(8,128)S(1)} %bitcast.65, f32[8,2048]{1,0:T(8,128)S(1)} %get-tuple-element.14, f32[256,2048]{1,0:T(8,128)S(1)} %bitcast.63), kind=kOutput, calls=%fused_computation.14 | convolution fusion | flops 2164785152 | bytes 9568256 | tf_op jit(solution)/shard_map/aj,bj->ab/dot_general | solution.py:47
  144.2 0.0 copy-start.2
  144.2 0.0 copy-start.3
  144.2 5.1 %all-to-all-start.2 = ((f32[16,128,256]{2,1,0:T(8,128)}), f32[16,128,256]{2,1,0:T(8,128)}, u32[]{:S(2)}, u32[]{:S(2)}) async-start(f32[16,128,256]{2,1,0:T(8,128)} %bitcast.61), calls=%async_computation.2 | async-start | bytes 4194304 | tf_op jit(solution)/shard_map/all_to_all | solution.py:48
  149.2 0.0 copy-done.2
  149.2 0.0 copy-done.3
  149.3 40.1 %all-gather = s32[16,16,2]{1,2,0:T(2,128)S(1)} all-gather(s32[1,16,2]{1,2,0:T(2,128)S(1)} %add_bitcast_fusion), channel_id=1, replica_groups=mesh['cls'=2,'dom'=16,'orient'=8] {'dom'}, dimensions={0}, use_global_device_ids=true | all-gather | bytes 2176 | tf_op jit(solution)/shard_map/all_gather | solution.py:27
  189.4 0.1 reshape.402
  189.5 0.1 mul.358
  189.6 0.1 copy.40
  189.7 0.1 mul.362
  189.8 0.1 copy.41
  189.9 8.7 %subtract_convert_fusion.1 = (bf16[1,16,16,2048]{3,1,2,0:T(8,128)(2,1)S(1)}, bf16[1,16,16,2048]{3,1,2,0:T(8,128)(2,1)S(1)}) fusion(f32[2048]{0:T(1024)S(1)} %get-tuple-element.23, f32[16,16]{0,1:T(8,128)S(1)} %copy.41, f32[2048]{0:T(1024)S(1)} %get-tuple-element.22, f32[16,16]{0,1:T(8,128)S(1)} %copy.40, bf16[2,16,16,2048]{3,1,2,0:T(8,128)(2,1)S(1)} %bitcast.58), kind=kLoop, calls=%fused_computation.18 | loop fusion | flops 7340032 | bytes 4212736 | tf_op jit(solution)/shard_map/convert_element_type | solution.py:64
  198.6 0.6 copy.42
  199.2 1.6 copy.44
  200.7 0.0 all-to-all-done.2
  200.7 1.7 reduce_sum.43
  202.5 0.1 copy.37
  202.6 0.1 reduce_max.10
  202.7 0.1 reduce_max.14
  202.8 0.1 reduce_max.18
  202.9 5.3 %pmax.7 = f32[16]{0:T(128)S(1)} all-reduce(f32[16]{0:T(128)S(1)} %reduce_max.18), channel_id=1, replica_groups=mesh['cls'=2,'dom'=16,'orient'=8] {'cls'}, use_global_device_ids=true, to_apply=%region_3.4 | all-reduce | flops 16 | bytes 128 | tf_op jit(solution)/shard_map/pmax | solution.py:53
  208.2 0.1 sub.78
  208.3 0.1 sub.79
  208.4 0.2 exponential_reduce_fusion.1
  208.5 0.1 reduce_sum.46
  208.6 0.1 reduce_sum.47
  208.8 5.3 %psum.7 = f32[16]{0:T(128)S(1)} all-reduce(f32[16]{0:T(128)S(1)} %reduce_sum.47), channel_id=1, replica_groups=mesh['cls'=2,'dom'=16,'orient'=8] {'cls'}, use_global_device_ids=true, to_apply=%region_7.8 | all-reduce | flops 16 | bytes 128 | tf_op jit(solution)/shard_map/psum | solution.py:56
  214.1 0.0 copy-start.1
  214.1 1.1 reshape.395
  215.2 0.5 exponential_reduce_fusion
  215.7 0.0 copy-done.1
  215.7 0.6 fusion.34
  216.3 18.2 %all-gather.1 = bf16[16,16,4]{1,2,0:T(4,128)(2,1)S(1)} all-gather(bf16[1,16,4]{1,2,0:T(4,128)(2,1)S(1)} %get-tuple-element.4), channel_id=1, replica_groups=mesh['cls'=2,'dom'=16,'orient'=8] {'dom'}, dimensions={0}, use_global_device_ids=true | all-gather | bytes 2176 | tf_op jit(solution)/shard_map/all_gather | solution.py:59
  234.6 0.1 reshape.404
  234.7 0.3 convolution_bitcast_fusion.1
  235.0 1.5 convolution_bitcast_fusion
  236.5 0.3 copy.46
  236.9 24.6 %all_to_all.30 = f32[8,2,4,2048]{3,2,1,0:T(4,128)S(1)} all-to-all(f32[8,2,4,2048]{3,2,1,0:T(4,128)S(1)} %copy.46), channel_id=1, replica_groups=mesh['cls'=2,'dom'=16,'orient'=8] {'orient'}, dimensions={0} | all-to-all | bytes 1048576 | tf_op jit(solution)/shard_map/all_to_all | solution.py:77
  261.5 0.1 reduce_sum.48
  261.6 0.7 broadcast_in_dim.2
  (13 shorter events, 0.2 us)
Async XLA Ops:
  2.1 60.7 %all-to-all-start.1 = ((bf16[8,2,4,8,256]{4,3,2,1,0:T(8,128)(2,1)}), bf16[8,2,4,8,256]{4,3,2,1,0:T(8,128)(2,1)S(1)}, u32[]{:S(2)}, u32[]{:S(2)}) async-start(bf16[8,2,4,8,256]{4,3,2,1,0:T(8,128)(2,1)} %stack.2), calls=%async_computation.1 | async-start | bytes 524288 | tf_op jit(solution)/shard_map/all_to_all | solution.py:25
  62.8 34.0 %all-to-all-start = ((bf16[16,2,32768]{2,1,0:T(2,128)(2,1)}), bf16[16,2,32768]{2,1,0:T(2,128)(2,1)S(1)}, u32[]{:S(2)}, u32[]{:S(2)}) async-start(bf16[16,2,32768]{2,1,0:T(2,128)(2,1)} %reshape.419), calls=%async_computation | async-start | bytes 4194304 | tf_op jit(solution)/shard_map/all_to_all | solution.py:23
  136.2 1.2 copy-start
  144.2 5.1 %copy-start.2 = (s32[16,1]{0,1:T(1,128)S(1)}, s32[16,1]{0,1:T(1,128)}, u32[]{:S(2)}) copy-start(s32[16,1]{0,1:T(1,128)} %param.8) | copy-start | bytes 196
  144.2 5.1 %copy-start.3 = (s32[16,1]{0,1:T(1,128)S(1)}, s32[16,1]{0,1:T(1,128)}, u32[]{:S(2)}) copy-start(s32[16,1]{0,1:T(1,128)} %param.7) | copy-start | bytes 196
  144.2 56.6 %all-to-all-start.2 = ((f32[16,128,256]{2,1,0:T(8,128)}), f32[16,128,256]{2,1,0:T(8,128)}, u32[]{:S(2)}, u32[]{:S(2)}) async-start(f32[16,128,256]{2,1,0:T(8,128)} %bitcast.61), calls=%async_computation.2 | async-start | bytes 4194304 | tf_op jit(solution)/shard_map/all_to_all | solution.py:48
  214.1 1.6 copy-start.1
